TPU v7x, 32 devices: a whole 2x2x4 slice. The times are simulated.
32 devices in a mesh: echo: 2 (over x), coil: 8 (over z, core), read: 2 (over y).
Axes of the slice: x: 2, y: 2, z: 4, core: 2. Of those that a mesh axis runs over, the one named last changes fastest.
Arguments:
- kspace: bfloat16 [384, 2, 8, 4, 2, 192], P(None, 'echo', 'coil', 'read'), may hold values from -3 to 3
- sampling: int32 [384, 2, 192], P(None, 'echo'), may hold values 0 or 1
- coil_maps: bfloat16 [384, 8, 4, 2, 192], P(None, 'coil', 'read'), may hold values from -1.5 to 1.5
- image: float32 [384, 2, 4, 2, 192], P('coil', 'echo', 'read'), may hold values from -6 to 6
- filters: bfloat16 [48, 3, 3, 3, 2], replicated, may hold values from -0.875 to 0.875
- thresholds: float32 [48], replicated, may hold values from 0.5 to 8
- dc_weight: float32 [2], P('echo'), may hold values from 0.5 to 2
Outputs:
- updated: float32 [384, 2, 4, 2, 192], P('coil', 'echo', 'read')
All inputs are finite; a program needn't handle non-finite values. No bound on the sum of `sampling` on one device may be relied on, other than what follows from the above.
Results may differ from a plain program's by a relative error of at most 0.0033.
Values may be sent and summed in bfloat16 or wider, within the bound.
A program may use at most 128 MiB of HBM per device.

v0:
```python
import functools

import numpy as np
import jax
import jax.numpy as jnp
from jax import lax
from jax.experimental import pallas as pl
from jax.experimental.pallas import tpu as pltpu
from jax.sharding import PartitionSpec as P

MESH = pl.DeviceIdType.MESH
F32 = jnp.float32
BF16 = jnp.bfloat16
SLAB = 32


def tables(length):
    product = np.outer(np.arange(length), np.arange(length)) % length
    phases = product * (2.0 * np.pi / length)
    normalize = length ** (-0.5)
    return np.cos(phases) * normalize, np.sin(phases) * normalize


def window_rows(rows, peers):
    for size in range(2, rows + 1):
        if rows % size == 0 and rows // size <= peers:
            return size
    return rows


def dot(left, right):
    return jnp.dot(left, right, preferred_element_type=F32)


def kernel(
    cfg,
    dc_ref, img_ref, xs_ref, kspace_hbm, maps_hbm, samp_hbm, fz_hbm, az_hbm, ty_hbm,
    wide_ref, tall_ref, thr_ref,
    adj_ref, pen_ref,
    gat, rs_send, rs_recv, ext, edge, pen_send, pen_recv, pacc, slab,
    kspace, maps, samp, fz, az, ty,
    local_sem, ag_send_sem, ag_recv_sem, x_send_sem, x_recv_sem, e_send_sem, e_recv_sem,
    p_send_sem, p_recv_sem, rs_send_sem, rs_recv_sem,
):
    n_e, n_c, n_r, n_q, rq, nz, ny = cfg
    peers = n_e * n_r
    e = lax.axis_index("echo")
    c = lax.axis_index("coil")
    r = lax.axis_index("read")
    q = e * n_r + r
    s_local, rb = rs_send.shape[0], img_ref.shape[0]
    width = 2 * nz
    zp = ext.shape[-1]

    loads = [
        pltpu.make_async_copy(src, dst, local_sem.at[i])
        for i, (src, dst) in enumerate(
            [(kspace_hbm, kspace), (maps_hbm, maps), (samp_hbm, samp), (fz_hbm, fz), (az_hbm, az), (ty_hbm, ty)]
        )
    ]

    def remote(src, dst, send, recv, target):
        return pltpu.make_async_remote_copy(
            src_ref=src, dst_ref=dst, send_sem=send, recv_sem=recv, device_id=target, device_id_type=MESH
        )

    def when(condition, act):
        if condition is True:
            act()
        else:
            pl.when(condition)(act)

    def up(d):
        return lax.rem(q + d, peers)

    def down(d):
        return lax.rem(q + peers - d, peers)

    def active(which):
        return True if n_q == peers else which < n_q

    barrier = pltpu.get_barrier_semaphore()
    for d in range(1, n_c):
        pl.semaphore_signal(barrier, inc=1, device_id=(e, lax.rem(c + d, n_c), r), device_id_type=MESH)
    for d in range(1, peers):
        pl.semaphore_signal(barrier, inc=1, device_id=(up(d) // n_r, c, lax.rem(up(d), n_r)), device_id_type=MESH)
        for step, ok in ((1, c < n_c - 1), (-1, c > 0)):
            @pl.when(ok)
            def _():
                pl.semaphore_signal(
                    barrier, inc=1, device_id=(up(d) // n_r, c + step, lax.rem(up(d), n_r)), device_id_type=MESH
                )
    sides = jnp.minimum(c, 1) + jnp.minimum(n_c - 1 - c, 1)
    pl.semaphore_wait(barrier, n_c - 1 + (peers - 1) * (1 + sides))

    def window(d):
        to = up(d)
        return remote(
            xs_ref.at[1 + to], ext.at[e, r], x_send_sem.at[d], x_recv_sem.at[d], (to // n_r, c, lax.rem(to, n_r))
        )

    last = n_q - 1
    edge_up = lambda: remote(
        xs_ref.at[n_q + 1], edge.at[e, r], e_send_sem.at[0], e_recv_sem.at[q], (0, c + 1, 0)
    )
    edge_down = lambda: remote(
        xs_ref.at[0], edge.at[e, r], e_send_sem.at[1], e_recv_sem.at[q], (last // n_r, c - 1, last % n_r)
    )
    for d in range(1, peers):
        when(active(up(d)), lambda: window(d).start())
    pl.when(c < n_c - 1)(lambda: edge_up().start())
    pl.when(c > 0)(lambda: edge_down().start())

    def gather(d):
        return remote(
            img_ref, gat.at[c], ag_send_sem.at[d], ag_recv_sem.at[d], (e, lax.rem(c + d, n_c), r)
        )

    for d in range(1, n_c):
        gather(d).start()
    for load in loads:
        load.start()
    gat[c] = img_ref[...]

    has_edge = jnp.logical_or(
        jnp.logical_and(q == 0, c > 0), jnp.logical_and(q == last, c < n_c - 1)
    )

    @pl.when(jnp.logical_not(has_edge))
    def _():
        edge[...] = jnp.zeros_like(edge)

    def regularize():
        ext[e, r] = xs_ref[1 + q]
        for d in range(1, peers):
            src = down(d)
            remote(
                xs_ref.at[0], ext.at[src // n_r, lax.rem(src, n_r)], x_send_sem.at[d], x_recv_sem.at[d], (e, c, r)
            ).wait_recv()

        @pl.when(has_edge)
        def _():
            for src in range(peers):
                remote(
                    xs_ref.at[0], edge.at[src // n_r, src % n_r], e_send_sem.at[0], e_recv_sem.at[src], (e, c, r)
                ).wait_recv()

        rows = rq + 4
        taps = 2 * s_local * n_r
        for echo in range(n_e):
            parts = [ext[echo, read].astype(F32) + edge[echo, read].astype(F32) for read in range(n_r)]
            block = jnp.concatenate(parts, axis=1) if n_r > 1 else parts[0]
            flat = block.reshape(rows * taps, zp)
            moved = [
                pltpu.roll(flat, 1, 1).reshape(rows, taps, zp),
                block,
                pltpu.roll(flat, zp - 1, 1).reshape(rows, taps, zp),
            ]
            fill = [jnp.zeros((rows, SLAB - 3 * taps, zp), F32)] if SLAB > 3 * taps else []
            slab[echo] = jnp.concatenate(moved + fill, axis=1).reshape(rows * SLAB, zp).astype(BF16)

        pacc[...] = jnp.zeros_like(pacc)
        tall = tall_ref[...]
        wide = wide_ref[...]
        lane_ok = lax.broadcasted_iota(jnp.int32, (1, zp), 1) < nz
        first = c * rb + q * rq - 1

        def row(i, carry):
            start = pl.multiple_of(i * SLAB, SLAB)
            response = [dot(tall, slab[echo, pl.ds(start, 3 * SLAB), :]) for echo in range(n_e)]
            energy = response[0] * response[0]
            for other in response[1:]:
                energy = energy + other * other
            magnitude = jnp.sqrt(energy)
            factor = magnitude / (magnitude + thr_ref[...])
            inside = jnp.logical_and(first + i >= 0, first + i < ny)
            factor = jnp.where(jnp.logical_and(lane_ok, inside), factor, 0.0)
            for echo in range(n_e):
                spread = dot(wide, (response[echo] * factor).astype(BF16))
                for a in range(3):
                    pacc[echo, i + a] += spread[a * SLAB : (a + 1) * SLAB]
            return carry

        lax.fori_loop(0, rq + 2, row, 0, unroll=2)
        for echo in range(n_e):
            held = pacc[echo, 2 : 2 + rq]
            low = pltpu.roll(held[:, :taps].reshape(rq * taps, zp), zp - 1, 1).reshape(rq, taps, zp)
            high = pltpu.roll(held[:, 2 * taps : 3 * taps].reshape(rq * taps, zp), 1, 1).reshape(rq, taps, zp)
            total = low + held[:, taps : 2 * taps] + high
            for read in range(n_r):
                pen_send[echo, read] = total[:, read * 2 * s_local : (read + 1) * 2 * s_local]
        pen_recv[q] = pen_send[e, r]

    def penalty_out(d):
        to = up(d)
        return remote(
            pen_send.at[to // n_r, lax.rem(to, n_r)], pen_recv.at[q], p_send_sem.at[d], p_recv_sem.at[d],
            (to // n_r, c, lax.rem(to, n_r)),
        )

    def all_penalties():
        regularize()
        for d in range(1, peers):
            penalty_out(d).start()

    when(active(q), all_penalties)

    for d in range(1, n_c):
        src = lax.rem(c + n_c - d, n_c)
        remote(img_ref, gat.at[src], ag_send_sem.at[d], ag_recv_sem.at[d], (e, c, r)).wait_recv()
    for load in loads:
        load.wait()

    def scatter(s, d):
        to = lax.rem(c + d, n_c)
        return remote(
            rs_send.at[s, to], rs_recv.at[s, c], rs_send_sem.at[s, d], rs_recv_sem.at[s, d], (e, to, r)
        )

    sampled = samp[...].astype(F32)
    for s in range(s_local):
        image = gat[:, :, s * width : (s + 1) * width].astype(F32).reshape(ny, width).T
        real, imag = image[:nz], image[nz:]
        map_real, map_imag = maps[s, 0].astype(F32), maps[s, 1].astype(F32)
        weighted = jnp.concatenate(
            [map_real * real - map_imag * imag, map_real * imag + map_imag * real], 0
        ).astype(BF16)
        halfway = dot(fz[...], weighted).astype(BF16)
        spectrum = dot(halfway, ty[...])
        spec_real = spectrum[:nz, :ny] + spectrum[nz:, ny:]
        spec_imag = spectrum[nz:, :ny] - spectrum[:nz, ny:]
        residual = jnp.concatenate(
            [
                sampled * (spec_real - kspace[s, 0].astype(F32)),
                sampled * (spec_imag - kspace[s, 1].astype(F32)),
            ],
            0,
        ).astype(BF16)
        returned = dot(residual, ty[...])
        backward = jnp.concatenate(
            [returned[:nz, :ny] - returned[nz:, ny:], returned[nz:, :ny] + returned[:nz, ny:]], 0
        ).astype(BF16)
        restored = dot(az[...], backward)
        back_real, back_imag = restored[:nz], restored[nz:]
        map_real, map_imag = maps[s, 0].astype(F32), maps[s, 1].astype(F32)
        adjoint = jnp.concatenate(
            [map_real * back_real + map_imag * back_imag, map_real * back_imag - map_imag * back_real], 0
        ).T
        rs_send[s] = adjoint.reshape(n_c, rb, width).astype(BF16)
        for d in range(1, n_c):
            scatter(s, d).start()

    for d in range(1, peers):
        src = down(d)
        when(
            active(src),
            lambda: remote(
                pen_send.at[0, 0], pen_recv.at[src], p_send_sem.at[d], p_recv_sem.at[d], (e, c, r)
            ).wait_recv(),
        )
    pen_ref[...] = pen_recv[...].reshape(rb, 2 * s_local, zp)

    dc = dc_ref[0]
    for s in range(s_local):
        total = rs_send[s, c].astype(F32)
        for d in range(1, n_c):
            src = lax.rem(c + n_c - d, n_c)
            remote(
                rs_send.at[s, src], rs_recv.at[s, src], rs_send_sem.at[s, d], rs_recv_sem.at[s, d], (e, c, r)
            ).wait_recv()
            total = total + rs_recv[s, src].astype(F32)
        adj_ref[:, s * width : (s + 1) * width] = dc * total

    for d in range(1, n_c):
        gather(d).wait_send()
        for s in range(s_local):
            scatter(s, d).wait_send()
    for d in range(1, peers):
        when(active(up(d)), lambda: window(d).wait_send())
        when(active(q), lambda: penalty_out(d).wait_send())
    pl.when(c < n_c - 1)(lambda: edge_up().wait_send())
    pl.when(c > 0)(lambda: edge_down().wait_send())


def body(kspace, sampling, coil_maps, image, filters, thresholds, dc_weight):
    n_e, n_c, n_r = lax.axis_size("echo"), lax.axis_size("coil"), lax.axis_size("read")
    rb, _, s_local, _, nz = image.shape
    ny = kspace.shape[0]
    peers = n_e * n_r
    rq = window_rows(rb, peers)
    n_q = rb // rq
    zp = -(-(nz + 1) // 128) * 128
    width = 2 * nz
    slices = s_local * n_r
    taps = 2 * slices
    count = filters.shape[0]

    col_cos, col_sin = tables(nz)
    row_cos, row_sin = tables(ny)
    fz = jnp.asarray(np.block([[col_cos, col_sin], [-col_sin, col_cos]]), BF16)
    az = jnp.asarray(np.block([[col_cos, -col_sin], [col_sin, col_cos]]), BF16)
    ty = jnp.asarray(np.concatenate([row_cos, row_sin], 1), BF16)

    rounded = image.astype(BF16)
    flat = rounded.reshape(rb, s_local * width)
    rows = rounded.reshape(rb, 2 * s_local, nz)
    margin = rq + 2
    padded = jnp.pad(rows, ((margin, margin), (0, 0), (0, zp - nz)))
    xs = jnp.stack([padded[j * rq : j * rq + rq + 4] for j in range(n_q + 2)])

    taps_of = jnp.transpose(filters, (1, 3, 2, 4, 0))
    shifted = jnp.stack(
        [
            jnp.pad(taps_of, ((0, 0), (0, 0), (at, slices - 1 - at), (0, 0), (0, 0)))[:, :, 1 : slices + 1]
            for at in range(slices)
        ],
        4,
    )
    wide = jnp.pad(
        shifted.reshape(3, 3 * taps, slices * count), ((0, 0), (0, SLAB - 3 * taps), (0, 0))
    ).reshape(3 * SLAB, slices * count)
    tall = wide.T
    thr = jnp.tile(thresholds, slices)[:, None]

    k_view = jnp.transpose(kspace[:, 0, 0], (1, 2, 3, 0))
    m_view = jnp.transpose(coil_maps[:, 0], (1, 2, 3, 0))
    s_view = jnp.transpose(sampling[:, 0], (1, 0))

    vmem = pl.BlockSpec(memory_space=pltpu.VMEM)
    hbm = pl.BlockSpec(memory_space=pl.ANY)
    smem = pl.BlockSpec(memory_space=pltpu.SMEM)
    dma = pltpu.SemaphoreType.DMA
    total, penalty = pl.pallas_call(
        functools.partial(kernel, (n_e, n_c, n_r, n_q, rq, nz, ny)),
        out_shape=(
            jax.ShapeDtypeStruct((rb, s_local * width), F32),
            jax.ShapeDtypeStruct((rb, 2 * s_local, zp), F32),
        ),
        in_specs=[smem, vmem, vmem, hbm, hbm, hbm, hbm, hbm, hbm, vmem, vmem, vmem],
        out_specs=(vmem, vmem),
        scratch_shapes=[
            pltpu.VMEM((n_c, rb, s_local * width), BF16),
            pltpu.VMEM((s_local, n_c, rb, width), BF16),
            pltpu.VMEM((s_local, n_c, rb, width), BF16),
            pltpu.VMEM((n_e, n_r, rq + 4, 2 * s_local, zp), BF16),
            pltpu.VMEM((n_e, n_r, rq + 4, 2 * s_local, zp), BF16),
            pltpu.VMEM((n_e, n_r, rq, 2 * s_local, zp), F32),
            pltpu.VMEM((n_q, rq, 2 * s_local, zp), F32),
            pltpu.VMEM((n_e, rq + 4, SLAB, zp), F32),
            pltpu.VMEM((n_e, (rq + 4) * SLAB, zp), BF16),
            pltpu.VMEM(k_view.shape, BF16),
            pltpu.VMEM(m_view.shape, BF16),
            pltpu.VMEM(s_view.shape, jnp.int32),
            pltpu.VMEM(fz.shape, BF16),
            pltpu.VMEM(az.shape, BF16),
            pltpu.VMEM(ty.shape, BF16),
            dma((6,)),
            dma((n_c,)), dma((n_c,)),
            dma((peers,)), dma((peers,)),
            dma((2,)), dma((peers,)),
            dma((peers,)), dma((peers,)),
            dma((s_local, n_c)), dma((s_local, n_c)),
        ],
        compiler_params=pltpu.CompilerParams(
            collective_id=0, has_side_effects=True, vmem_limit_bytes=56 << 20
        ),
        name="cascade",
    )(dc_weight, flat, xs, k_view, m_view, s_view, fz, az, ty, wide, tall, thr)
    shape = image.shape
    return image - total.reshape(shape) - penalty[:, :, :nz].reshape(shape)


def solution(mesh):
    return jax.shard_map(
        body,
        mesh=mesh,
        in_specs=(
            P(None, "echo", "coil", "read", None, None),
            P(None, "echo", None),
            P(None, "coil", "read", None, None),
            P("coil", "echo", "read", None, None),
            P(),
            P(),
            P("echo"),
        ),
        out_specs=P("coil", "echo", "read", None, None),
        check_vma=False,
    )
```

profile of v0, /device:TPU:25, one launch (start us, length us, event | category | flops | bytes accessed | tf_op | source)
XLA Modules:
  0.0 43.4 jit_solution(3617939411854645194)
XLA Ops:
  0.7 0.0 copy-start.4
  0.7 0.6 %copy-done.4 = f32[48]{0:T(128)S(1)} copy-done((f32[48]{0:T(128)S(1)}, f32[48]{0:T(128)}, u32[]{:S(2)}) %copy-start.4) | copy-done | bytes 216
  1.3 0.9 %fusion.12 = (bf16[3,3,4,2,1,48]{5,3,1,2,0,4:T(2,128)(2,1)S(1)}, bf16[3,3,4,2,1,48]{5,3,1,2,0,4:T(2,128)(2,1)S(1)}, bf16[3,3,4,2,1,48]{5,3,1,2,0,4:T(2,128)(2,1)S(1)}, bf16[3,3,4,2,1,48]{5,3,1,2,0,4:T(2,128)(2,1)S(1)}) fusion(bf16[3,3,3,2,48]{4,3,1,2,0:T(2,128)(2,1)} %bitcast.58), kind=kLoop, calls=%fused_computation.25 | loop fusion | bytes 32832 | tf_op jit(solution)/shard_map/stack | solution.py:312
  2.2 0.1 pad_maximum_fusion
  2.4 0.0 copy-start
  2.4 0.1 reshape.21
  2.6 0.0 copy-start.1
  2.6 0.7 %copy.15 = bf16[96,192]{0,1:T(8,128)(2,1)} copy(bf16[96,192]{1,0:T(8,128)(2,1)S(1)} %bitcast.53) | data formatting | bytes 73728 | tf_op jit(solution)/shard_map/reshape | solution.py:321
  3.3 0.0 copy-done.1
  3.3 0.8 %broadcast_in_dim_tile.4.thr_ref = f32[192,1]{1,0:T(8,128)} reshape(f32[4,48]{1,0:T(4,128)S(1)} %tile.2) | data formatting | bytes 1536 | tf_op jit(solution)/shard_map/broadcast_in_dim;tile | solution.py:323
  4.0 0.0 copy-done
  4.1 0.1 convert_element_type.15
  4.1 0.7 %reshape.19.img_ref = bf16[48,768]{1,0:T(8,128)(2,1)} reshape(bf16[48,1,2,2,192]{4,3,2,1,0:T(2,128)(2,1)S(1)} %convert_element_type.15) | data formatting | bytes 147456 | tf_op jit(solution)/shard_map/reshape | solution.py:305
  4.9 0.1 reshape.20
  5.1 0.0 copy-start.2
  5.1 0.7 %copy-done.2 = bf16[6,16,4,256]{3,2,1,0:T(4,128)(2,1)} copy-done((bf16[6,16,4,256]{3,2,1,0:T(4,128)(2,1)}, bf16[6,16,4,256]{3,2,1,0:T(4,128)(2,1)S(1)}, u32[]{:S(2)}) %copy-start.2) | copy-done | bytes 196632
  5.8 35.4 %cascade.1 = (f32[48,768]{1,0:T(8,128)}, f32[48,4,256]{2,1,0:T(4,128)}) custom-call(f32[1]{0:T(128)S(6)} %copy.24.dc_ref, bf16[48,768]{1,0:T(8,128)(2,1)} %reshape.19.img_ref, bf16[6,16,4,256]{3,2,1,0:T(4,128)(2,1)} %copy-done.2, bf16[2,2,192,384]{3,2,1,0:T(8,128)(2,1)} %bitcast.51, bf16[2,2,192,384]{3,2,1,0:T(8,128)(2,1)} %bitcast.52, s32[192,384]{1,0:T(8,128)} %bitcast.55, ...), custom_call_target="tpu_custom_call" | custom-call | tf_op jit(solution)/shard_map/cascade/pallas_call | solution.py:333
  41.2 0.0 copy-start.3
  41.2 1.1 %reshape.24 = f32[48,1,2,2,192]{4,3,2,0,1:T(2,128)S(1)} reshape(f32[48,4,192]{2,1,0:T(4,128)} %bitcast.56) | data formatting | bytes 294912 | tf_op jit(solution)/shard_map/reshape | solution.py:370
  42.3 0.0 copy-done.3
  42.4 0.2 reshape.23
  42.5 0.8 %bitcast_subtract_fusion = f32[48,1,2,2,192]{4,3,2,1,0:T(2,128)} fusion(f32[48,1,2,2,192]{4,3,2,0,1:T(2,128)S(1)} %reshape.24, f32[48,1,2,2,192]{4,3,2,1,0:T(2,128)S(1)} %copy-done, f32[48,1,2,2,192]{4,3,2,0,1:T(2,128)S(1)} %reshape.23), kind=kLoop, calls=%fused_computation | loop fusion | flops 73728 | bytes 589824 | tf_op jit(solution)/shard_map/sub | solution.py:370
  (9 shorter events, 0.2 us)
Async XLA Ops:
  0.7 0.7 %copy-start.4 = (f32[48]{0:T(128)S(1)}, f32[48]{0:T(128)}, u32[]{:S(2)}) copy-start(f32[48]{0:T(128)} %param.15) | copy-start | bytes 580
  2.4 1.6 %copy-start = (f32[48,1,2,2,192]{4,3,2,1,0:T(2,128)S(1)}, f32[48,1,2,2,192]{4,3,2,1,0:T(2,128)}, u32[]{:S(2)}) copy-start(f32[48,1,2,2,192]{4,3,2,1,0:T(2,128)} %param.13) | copy-start | bytes 442372
  2.6 0.7 %copy-start.1 = (bf16[3,32,192]{2,1,0:T(8,128)(2,1)}, bf16[3,32,192]{2,1,0:T(8,128)(2,1)S(1)}, u32[]{:S(2)}) copy-start(bf16[3,32,192]{2,1,0:T(8,128)(2,1)S(1)} %pad.29) | copy-start | bytes 110596
  5.1 0.7 %copy-start.2 = (bf16[6,16,4,256]{3,2,1,0:T(4,128)(2,1)}, bf16[6,16,4,256]{3,2,1,0:T(4,128)(2,1)S(1)}, u32[]{:S(2)}) copy-start(bf16[6,16,4,256]{3,2,1,0:T(4,128)(2,1)S(1)} %fusion.11.xs_ref) | copy-start | bytes 589828
  41.2 1.1 %copy-start.3 = (f32[48,768]{1,0:T(8,128)S(1)}, f32[48,768]{1,0:T(8,128)}, u32[]{:S(2)}) copy-start(f32[48,768]{1,0:T(8,128)} %get-tuple-element.7) | copy-start | bytes 442372
where the time goes:
time: 43.6 us; the launch traced here: 43.4 us
  Pallas kernels  35.4 us (81%)
  local copies, waits for them, and re-layouts  6.14 us (14%)
  other arithmetic  1.03 us (2%)
  between operations  0.8 us (2%)
    pallas_call x1, Pallas kernels, body(): pl.pallas_call(functools.partial(kernel, (n_e, n_c, n_r, n_q, rq, nz, ny)...  35.4 us
    unnamed x15, local copies, waits for them, and re-layouts  1.46 us
    reshape x2, local copies, waits for them, and re-layouts, body(): return image - total.reshape(shape) - penalty[:, :, :nz].reshape(shape)  1.3 us
    another operation x2, local copies, waits for them, and re-layouts, body(): jnp.stack([jnp.pad(taps_of, ((0, 0), (0, 0), (at, slices - 1 - at), (0, 0...  0.95 us

commit v1 on v0

--- a/solution.py
+++ b/solution.py
@@ -35,12 +35,12 @@
 def kernel(
     cfg,
     dc_ref, img_ref, xs_ref, kspace_hbm, maps_hbm, samp_hbm, fz_hbm, az_hbm, ty_hbm,
-    wide_ref, tall_ref, thr_ref,
+    filters_ref, spread_ref, thr_ref,
     adj_ref, pen_ref,
-    gat, rs_send, rs_recv, ext, edge, pen_send, pen_recv, pacc, slab,
+    gat, part, paired, rs_send, rs_recv, wide_ref, tall_ref, level, ext, edge, pen_send, pen_recv, pacc, slab,
     kspace, maps, samp, fz, az, ty,
     local_sem, ag_send_sem, ag_recv_sem, x_send_sem, x_recv_sem, e_send_sem, e_recv_sem,
-    p_send_sem, p_recv_sem, rs_send_sem, rs_recv_sem,
+    p_send_sem, p_recv_sem, rs_send_sem, rs_recv_sem, f_send_sem, f_recv_sem, pair_send_sem, pair_recv_sem,
 ):
     n_e, n_c, n_r, n_q, rq, nz, ny = cfg
     peers = n_e * n_r
@@ -49,6 +49,10 @@
     r = lax.axis_index("read")
     q = e * n_r + r
     s_local, rb = rs_send.shape[0], img_ref.shape[0]
+    chips = n_c // 2
+    core = lax.rem(c, 2)
+    chip = c // 2
+    partner = c + 1 - 2 * core
     width = 2 * nz
     zp = ext.shape[-1]
 
@@ -80,10 +84,12 @@
         return True if n_q == peers else which < n_q
 
     barrier = pltpu.get_barrier_semaphore()
-    for d in range(1, n_c):
-        pl.semaphore_signal(barrier, inc=1, device_id=(e, lax.rem(c + d, n_c), r), device_id_type=MESH)
-    for d in range(1, peers):
-        pl.semaphore_signal(barrier, inc=1, device_id=(up(d) // n_r, c, lax.rem(up(d), n_r)), device_id_type=MESH)
+    for d in range(chips):
+        to = lax.rem(c + 2 * d, n_c) if d else partner
+        pl.semaphore_signal(barrier, inc=1, device_id=(e, to, r), device_id_type=MESH)
+    for d in range(peers):
+        if d:
+            pl.semaphore_signal(barrier, inc=1, device_id=(up(d) // n_r, c, lax.rem(up(d), n_r)), device_id_type=MESH)
         for step, ok in ((1, c < n_c - 1), (-1, c > 0)):
             @pl.when(ok)
             def _():
@@ -91,7 +97,7 @@
                     barrier, inc=1, device_id=(up(d) // n_r, c + step, lax.rem(up(d), n_r)), device_id_type=MESH
                 )
     sides = jnp.minimum(c, 1) + jnp.minimum(n_c - 1 - c, 1)
-    pl.semaphore_wait(barrier, n_c - 1 + (peers - 1) * (1 + sides))
+    pl.semaphore_wait(barrier, chips + peers - 1 + peers * sides)
 
     def window(d):
         to = up(d)
@@ -112,15 +118,30 @@
     pl.when(c > 0)(lambda: edge_down().start())
 
     def gather(d):
-        return remote(
-            img_ref, gat.at[c], ag_send_sem.at[d], ag_recv_sem.at[d], (e, lax.rem(c + d, n_c), r)
-        )
-
-    for d in range(1, n_c):
+        to = lax.rem(c + 2 * d, n_c) if d else partner
+        return remote(img_ref, gat.at[c], ag_send_sem.at[d], ag_recv_sem.at[d], (e, to, r))
+
+    def forward(d):
+        src = lax.rem(c + n_c - 2 * d, n_c)
+        return remote(gat.at[src], gat.at[src], f_send_sem.at[d], f_recv_sem.at[d], (e, partner, r))
+
+    for d in range(chips):
         gather(d).start()
     for load in loads:
         load.start()
     gat[c] = img_ref[...]
+
+    count = filters_ref.shape[-1]
+    slices = s_local * n_r
+    flat_filters = filters_ref[...]
+    pieces = [dot(spread_ref[at], flat_filters) for at in range(slices)]
+    for at in range(slices):
+        wide_ref[:, at * count : (at + 1) * count] = pieces[at].astype(BF16)
+        tall_ref[at * count : (at + 1) * count, :] = pieces[at].T.astype(BF16)
+    shape = (slices, count, count)
+    on = lax.broadcasted_iota(jnp.int32, shape, 1) == lax.broadcasted_iota(jnp.int32, shape, 2)
+    column = jnp.sum(jnp.where(on, thr_ref[...].reshape(1, 1, count), 0.0), axis=2, keepdims=True)
+    level[...] = jnp.broadcast_to(column, (slices, count, zp)).reshape(slices * count, zp)
 
     has_edge = jnp.logical_or(
         jnp.logical_and(q == 0, c > 0), jnp.logical_and(q == last, c < n_c - 1)
@@ -172,7 +193,7 @@
             for other in response[1:]:
                 energy = energy + other * other
             magnitude = jnp.sqrt(energy)
-            factor = magnitude / (magnitude + thr_ref[...])
+            factor = magnitude / (magnitude + level[...])
             inside = jnp.logical_and(first + i >= 0, first + i < ny)
             factor = jnp.where(jnp.logical_and(lane_ok, inside), factor, 0.0)
             for echo in range(n_e):
@@ -205,17 +226,34 @@
 
     when(active(q), all_penalties)
 
-    for d in range(1, n_c):
-        src = lax.rem(c + n_c - d, n_c)
-        remote(img_ref, gat.at[src], ag_send_sem.at[d], ag_recv_sem.at[d], (e, c, r)).wait_recv()
+    for d in range(1, chips):
+        src = lax.rem(c + n_c - 2 * d, n_c)
+        remote(img_ref, gat.at[src], ag_send_sem.at[d], ag_recv_sem.at[d], (e, partner, r)).wait_recv()
+        forward(d).start()
+    remote(img_ref, gat.at[partner], ag_send_sem.at[0], ag_recv_sem.at[0], (e, partner, r)).wait_recv()
+    for d in range(1, chips):
+        src = lax.rem(partner + n_c - 2 * d, n_c)
+        remote(gat.at[src], gat.at[src], f_send_sem.at[d], f_recv_sem.at[d], (e, partner, r)).wait_recv()
     for load in loads:
         load.wait()
 
+    def pair(s):
+        return remote(
+            part.at[s, :, 1 - core], paired.at[s], pair_send_sem.at[s], pair_recv_sem.at[s], (e, partner, r)
+        )
+
     def scatter(s, d):
-        to = lax.rem(c + d, n_c)
+        to = lax.rem(chip + d, chips)
         return remote(
-            rs_send.at[s, to], rs_recv.at[s, c], rs_send_sem.at[s, d], rs_recv_sem.at[s, d], (e, to, r)
-        )
+            rs_send.at[s, to], rs_recv.at[s, chip], rs_send_sem.at[s, d], rs_recv_sem.at[s, d],
+            (e, 2 * to + core, r),
+        )
+
+    def send_sums(s):
+        pair(s).wait_recv()
+        rs_send[s] = (part[s, :, core].astype(F32) + paired[s].astype(F32)).astype(BF16)
+        for d in range(1, chips):
+            scatter(s, d).start()
 
     sampled = samp[...].astype(F32)
     for s in range(s_local):
@@ -227,6 +265,8 @@
         ).astype(BF16)
         halfway = dot(fz[...], weighted).astype(BF16)
         spectrum = dot(halfway, ty[...])
+        if s:
+            send_sums(s - 1)
         spec_real = spectrum[:nz, :ny] + spectrum[nz:, ny:]
         spec_imag = spectrum[nz:, :ny] - spectrum[:nz, ny:]
         residual = jnp.concatenate(
@@ -246,9 +286,9 @@
         adjoint = jnp.concatenate(
             [map_real * back_real + map_imag * back_imag, map_real * back_imag - map_imag * back_real], 0
         ).T
-        rs_send[s] = adjoint.reshape(n_c, rb, width).astype(BF16)
-        for d in range(1, n_c):
-            scatter(s, d).start()
+        part[s] = adjoint.reshape(chips, 2, rb, width).astype(BF16)
+        pair(s).start()
+    send_sums(s_local - 1)
 
     for d in range(1, peers):
         src = down(d)
@@ -262,19 +302,23 @@
 
     dc = dc_ref[0]
     for s in range(s_local):
-        total = rs_send[s, c].astype(F32)
-        for d in range(1, n_c):
-            src = lax.rem(c + n_c - d, n_c)
+        total = part[s, chip, core].astype(F32) + paired[s, chip].astype(F32)
+        for d in range(1, chips):
+            src = lax.rem(chip + chips - d, chips)
             remote(
-                rs_send.at[s, src], rs_recv.at[s, src], rs_send_sem.at[s, d], rs_recv_sem.at[s, d], (e, c, r)
+                rs_send.at[s, src], rs_recv.at[s, src], rs_send_sem.at[s, d], rs_recv_sem.at[s, d], (e, partner, r)
             ).wait_recv()
             total = total + rs_recv[s, src].astype(F32)
         adj_ref[:, s * width : (s + 1) * width] = dc * total
 
-    for d in range(1, n_c):
+    for d in range(chips):
         gather(d).wait_send()
-        for s in range(s_local):
-            scatter(s, d).wait_send()
+        if d:
+            forward(d).wait_send()
+            for s in range(s_local):
+                scatter(s, d).wait_send()
+    for s in range(s_local):
+        pair(s).wait_send()
     for d in range(1, peers):
         when(active(up(d)), lambda: window(d).wait_send())
         when(active(q), lambda: penalty_out(d).wait_send())
@@ -308,19 +352,17 @@
     padded = jnp.pad(rows, ((margin, margin), (0, 0), (0, zp - nz)))
     xs = jnp.stack([padded[j * rq : j * rq + rq + 4] for j in range(n_q + 2)])
 
-    taps_of = jnp.transpose(filters, (1, 3, 2, 4, 0))
-    shifted = jnp.stack(
-        [
-            jnp.pad(taps_of, ((0, 0), (0, 0), (at, slices - 1 - at), (0, 0), (0, 0)))[:, :, 1 : slices + 1]
-            for at in range(slices)
-        ],
-        4,
-    )
-    wide = jnp.pad(
-        shifted.reshape(3, 3 * taps, slices * count), ((0, 0), (0, SLAB - 3 * taps), (0, 0))
-    ).reshape(3 * SLAB, slices * count)
-    tall = wide.T
-    thr = jnp.tile(thresholds, slices)[:, None]
+    spread = np.zeros((slices, 3, SLAB, 3, 3, 3, 2))
+    for at in range(slices):
+        for a in range(3):
+            for b in range(3):
+                for d in range(3):
+                    for p in range(2):
+                        if 0 <= at + b - 1 < slices:
+                            spread[at, a, d * taps + (at + b - 1) * 2 + p, a, b, d, p] = 1.0
+    spread = jnp.asarray(spread.reshape(slices, 3 * SLAB, 54), BF16)
+    flat_filters = filters.reshape(count, 54).T
+    thr = thresholds[None, :]
 
     k_view = jnp.transpose(kspace[:, 0, 0], (1, 2, 3, 0))
     m_view = jnp.transpose(coil_maps[:, 0], (1, 2, 3, 0))
@@ -340,8 +382,13 @@
         out_specs=(vmem, vmem),
         scratch_shapes=[
             pltpu.VMEM((n_c, rb, s_local * width), BF16),
-            pltpu.VMEM((s_local, n_c, rb, width), BF16),
-            pltpu.VMEM((s_local, n_c, rb, width), BF16),
+            pltpu.VMEM((s_local, n_c // 2, 2, rb, width), BF16),
+            pltpu.VMEM((s_local, n_c // 2, rb, width), BF16),
+            pltpu.VMEM((s_local, n_c // 2, rb, width), BF16),
+            pltpu.VMEM((s_local, n_c // 2, rb, width), BF16),
+            pltpu.VMEM((3 * SLAB, slices * count), BF16),
+            pltpu.VMEM((slices * count, 3 * SLAB), BF16),
+            pltpu.VMEM((slices * count, zp), F32),
             pltpu.VMEM((n_e, n_r, rq + 4, 2 * s_local, zp), BF16),
             pltpu.VMEM((n_e, n_r, rq + 4, 2 * s_local, zp), BF16),
             pltpu.VMEM((n_e, n_r, rq, 2 * s_local, zp), F32),
@@ -360,12 +407,13 @@
             dma((2,)), dma((peers,)),
             dma((peers,)), dma((peers,)),
             dma((s_local, n_c)), dma((s_local, n_c)),
+            dma((n_c,)), dma((n_c,)), dma((s_local,)), dma((s_local,)),
         ],
         compiler_params=pltpu.CompilerParams(
             collective_id=0, has_side_effects=True, vmem_limit_bytes=56 << 20
         ),
         name="cascade",
-    )(dc_weight, flat, xs, k_view, m_view, s_view, fz, az, ty, wide, tall, thr)
+    )(dc_weight, flat, xs, k_view, m_view, s_view, fz, az, ty, flat_filters, spread, thr)
     shape = image.shape
     return image - total.reshape(shape) - penalty[:, :, :nz].reshape(shape)
 

time: 43.6 us -> 38.3 us (0.88)
  the two profiles are of different devices: /device:TPU:25 before, /device:TPU:0 now
where the time goes in v1:
time: 38.3 us; the launch traced here: 38.1 us
  Pallas kernels  30.5 us (80%)
  local copies, waits for them, and re-layouts  5.02 us (13%)
  other arithmetic  1.81 us (5%)
  between operations  0.74 us (2%)
    pallas_call x1, Pallas kernels, body(): pl.pallas_call(functools.partial(kernel, (n_e, n_c, n_r, n_q, rq, nz, ny)...  30.5 us
    unnamed x11, local copies, waits for them, and re-layouts  1.53 us
    reshape x1, local copies, waits for them, and re-layouts, body(): flat_filters = filters.reshape(count, 54).T  1.33 us
    reshape x2, local copies, waits for them, and re-layouts, body(): return image - total.reshape(shape) - penalty[:, :, :nz].reshape(shape)  1.3 us
    convert_element_type x1, other arithmetic, body(): rounded = image.astype(BF16)  0.99 us
    sub x1, other arithmetic, body(): return image - total.reshape(shape) - penalty[:, :, :nz].reshape(shape)  0.81 us

profile of v1, /device:TPU:0, one launch (start us, length us, event | category | flops | bytes accessed | tf_op | source)
XLA Modules:
  0.0 38.1 jit_solution(4788839753948088613)
XLA Ops:
  0.7 1.3 %reshape.17 = bf16[48,54]{0,1:T(8,128)(2,1)} reshape(bf16[48,3,3,3,2]{0,4,3,2,1:T(2,128)(2,1)} %param.15) | data formatting | bytes 10368 | tf_op jit(solution)/shard_map/reshape | solution.py:364
  2.0 1.0 %convert_element_type.5 = bf16[48,1,2,2,192]{4,3,2,1,0:T(2,128)(2,1)S(1)} convert(f32[48,1,2,2,192]{4,3,2,1,0:T(2,128)} %param.14) | non-fusion elementwise | flops 36864 | bytes 221184 | tf_op jit(solution)/shard_map/convert_element_type | solution.py:348
  3.0 0.7 %reshape.15.img_ref = bf16[48,768]{1,0:T(8,128)(2,1)} reshape(bf16[48,1,2,2,192]{4,3,2,1,0:T(2,128)(2,1)S(1)} %convert_element_type.5) | data formatting | bytes 147456 | tf_op jit(solution)/shard_map/reshape | solution.py:349
  3.7 0.1 reshape.16
  4.0 0.0 copy-start.1
  4.0 0.7 %copy-done.1 = bf16[6,16,4,256]{3,2,1,0:T(4,128)(2,1)} copy-done((bf16[6,16,4,256]{3,2,1,0:T(4,128)(2,1)}, bf16[6,16,4,256]{3,2,1,0:T(4,128)(2,1)S(1)}, u32[]{:S(2)}) %copy-start.1) | copy-done | bytes 196632
  4.7 30.5 %cascade.1 = (f32[48,768]{1,0:T(8,128)}, f32[48,4,256]{2,1,0:T(4,128)}) custom-call(f32[1]{0:T(128)S(6)} %copy.21.dc_ref, bf16[48,768]{1,0:T(8,128)(2,1)} %reshape.15.img_ref, bf16[6,16,4,256]{3,2,1,0:T(4,128)(2,1)} %copy-done.1, bf16[2,2,192,384]{3,2,1,0:T(8,128)(2,1)} %bitcast.44, bf16[2,2,192,384]{3,2,1,0:T(8,128)(2,1)} %bitcast.45, s32[192,384]{1,0:T(8,128)} %bitcast.46, ...), custom_call_target="tpu_custom_call" | custom-call | tf_op jit(solution)/shard_map/cascade/pallas_call | solution.py:375
  35.2 0.0 copy-start.2
  35.2 1.1 %reshape.19 = f32[48,1,2,2,192]{4,3,2,0,1:T(2,128)S(1)} reshape(f32[48,4,192]{2,1,0:T(4,128)} %bitcast.47) | data formatting | bytes 294912 | tf_op jit(solution)/shard_map/reshape | solution.py:418
  36.3 0.0 copy-done.2
  36.3 0.0 copy-start
  36.3 0.2 reshape.18
  36.5 0.7 %copy-done = f32[48,1,2,2,192]{4,3,2,1,0:T(2,128)S(1)} copy-done((f32[48,1,2,2,192]{4,3,2,1,0:T(2,128)S(1)}, f32[48,1,2,2,192]{4,3,2,1,0:T(2,128)}, u32[]{:S(2)}) %copy-start) | copy-done | bytes 147480
  37.3 0.8 %bitcast_subtract_fusion = f32[48,1,2,2,192]{4,3,2,1,0:T(2,128)} fusion(f32[48,1,2,2,192]{4,3,2,0,1:T(2,128)S(1)} %reshape.19, f32[48,1,2,2,192]{4,3,2,1,0:T(2,128)S(1)} %copy-done, f32[48,1,2,2,192]{4,3,2,0,1:T(2,128)S(1)} %reshape.18), kind=kLoop, calls=%fused_computation | loop fusion | flops 73728 | bytes 589824 | tf_op jit(solution)/shard_map/sub | solution.py:418
  (6 shorter events, 0.1 us)
Async XLA Ops:
  4.0 0.7 %copy-start.1 = (bf16[6,16,4,256]{3,2,1,0:T(4,128)(2,1)}, bf16[6,16,4,256]{3,2,1,0:T(4,128)(2,1)S(1)}, u32[]{:S(2)}) copy-start(bf16[6,16,4,256]{3,2,1,0:T(4,128)(2,1)S(1)} %fusion.11.xs_ref) | copy-start | bytes 589828
  35.2 1.1 %copy-start.2 = (f32[48,768]{1,0:T(8,128)S(1)}, f32[48,768]{1,0:T(8,128)}, u32[]{:S(2)}) copy-start(f32[48,768]{1,0:T(8,128)} %get-tuple-element.7) | copy-start | bytes 442372
  36.3 0.9 %copy-start = (f32[48,1,2,2,192]{4,3,2,1,0:T(2,128)S(1)}, f32[48,1,2,2,192]{4,3,2,1,0:T(2,128)}, u32[]{:S(2)}) copy-start(f32[48,1,2,2,192]{4,3,2,1,0:T(2,128)} %param.14) | copy-start | bytes 442372

commit v2 on v1

--- a/solution.py
+++ b/solution.py
@@ -12,6 +12,7 @@
 F32 = jnp.float32
 BF16 = jnp.bfloat16
 SLAB = 32
+GRANT = 24 << 20
 
 
 def tables(length):
@@ -133,7 +134,7 @@
 
     count = filters_ref.shape[-1]
     slices = s_local * n_r
-    flat_filters = filters_ref[...]
+    flat_filters = filters_ref[...].astype(F32).reshape(-1, count).astype(BF16)
     pieces = [dot(spread_ref[at], flat_filters) for at in range(slices)]
     for at in range(slices):
         wide_ref[:, at * count : (at + 1) * count] = pieces[at].astype(BF16)
@@ -151,7 +152,7 @@
     def _():
         edge[...] = jnp.zeros_like(edge)
 
-    def regularize():
+    def prepare():
         ext[e, r] = xs_ref[1 + q]
         for d in range(1, peers):
             src = down(d)
@@ -181,6 +182,8 @@
             slab[echo] = jnp.concatenate(moved + fill, axis=1).reshape(rows * SLAB, zp).astype(BF16)
 
         pacc[...] = jnp.zeros_like(pacc)
+
+    def respond(begin, end):
         tall = tall_ref[...]
         wide = wide_ref[...]
         lane_ok = lax.broadcasted_iota(jnp.int32, (1, zp), 1) < nz
@@ -202,7 +205,10 @@
                     pacc[echo, i + a] += spread[a * SLAB : (a + 1) * SLAB]
             return carry
 
-        lax.fori_loop(0, rq + 2, row, 0, unroll=2)
+        lax.fori_loop(begin, end, row, 0, unroll=True)
+
+    def collect():
+        taps = 2 * s_local * n_r
         for echo in range(n_e):
             held = pacc[echo, 2 : 2 + rq]
             low = pltpu.roll(held[:, :taps].reshape(rq * taps, zp), zp - 1, 1).reshape(rq, taps, zp)
@@ -219,12 +225,19 @@
             (to // n_r, c, lax.rem(to, n_r)),
         )
 
-    def all_penalties():
-        regularize()
+    split = (rq + 2) * 2 // 3
+
+    def before():
+        prepare()
+        respond(0, split)
+
+    def after():
+        respond(split, rq + 2)
+        collect()
         for d in range(1, peers):
             penalty_out(d).start()
 
-    when(active(q), all_penalties)
+    when(active(q), before)
 
     for d in range(1, chips):
         src = lax.rem(c + n_c - 2 * d, n_c)
@@ -289,6 +302,7 @@
         part[s] = adjoint.reshape(chips, 2, rb, width).astype(BF16)
         pair(s).start()
     send_sums(s_local - 1)
+    when(active(q), after)
 
     for d in range(1, peers):
         src = down(d)
@@ -361,15 +375,18 @@
                         if 0 <= at + b - 1 < slices:
                             spread[at, a, d * taps + (at + b - 1) * 2 + p, a, b, d, p] = 1.0
     spread = jnp.asarray(spread.reshape(slices, 3 * SLAB, 54), BF16)
-    flat_filters = filters.reshape(count, 54).T
+    flat_filters = jnp.transpose(filters, (1, 2, 3, 4, 0))
     thr = thresholds[None, :]
 
     k_view = jnp.transpose(kspace[:, 0, 0], (1, 2, 3, 0))
     m_view = jnp.transpose(coil_maps[:, 0], (1, 2, 3, 0))
     s_view = jnp.transpose(sampling[:, 0], (1, 0))
 
+    k_view, m_view, s_view, fz, az, ty = (
+        pltpu.with_memory_space_constraint(x, pltpu.HBM) for x in (k_view, m_view, s_view, fz, az, ty)
+    )
     vmem = pl.BlockSpec(memory_space=pltpu.VMEM)
-    hbm = pl.BlockSpec(memory_space=pl.ANY)
+    hbm = pl.BlockSpec(memory_space=pltpu.HBM)
     smem = pl.BlockSpec(memory_space=pltpu.SMEM)
     dma = pltpu.SemaphoreType.DMA
     total, penalty = pl.pallas_call(
@@ -410,7 +427,7 @@
             dma((n_c,)), dma((n_c,)), dma((s_local,)), dma((s_local,)),
         ],
         compiler_params=pltpu.CompilerParams(
-            collective_id=0, has_side_effects=True, vmem_limit_bytes=56 << 20
+            collective_id=0, has_side_effects=True, vmem_limit_bytes=GRANT
         ),
         name="cascade",
     )(dc_weight, flat, xs, k_view, m_view, s_view, fz, az, ty, flat_filters, spread, thr)

time: 38.3 us -> 31.1 us (0.81)
  Pallas kernels: 30.5 us -> 26 us
  local copies, waits for them, and re-layouts: 5.02 us -> 2.28 us
    pallas_call x1, Pallas kernels: 30.5 us -> 26 us  [body(): pl.pallas_call(functools.partial(kernel, (n_e, n_c, n_r, n_q, rq, nz, ny)...]
    reshape x1 -> x0, local copies, waits for them, and re-layouts: 1.33 us -> none  [body(): flat_filters = filters.reshape(count, 54).T]
    reshape x2, local copies, waits for them, and re-layouts: 1.3 us -> 0.34 us  [body(): return image - total.reshape(shape) - penalty[:, :, :nz].reshape(shape)]
    reshape x1, local copies, waits for them, and re-layouts: 0.74 us -> 0.12 us  [body(): flat = rounded.reshape(rb, s_local * width)]
    unnamed x11 -> x13, local copies, waits for them, and re-layouts: 1.53 us -> 1.71 us
where the time goes in v2:
time: 31.1 us; the launch traced here: 30.9 us
  Pallas kernels  26 us (84%)
  local copies, waits for them, and re-layouts  2.28 us (7%)
  other arithmetic  1.84 us (6%)
  between operations  0.75 us (2%)
    pallas_call x1, Pallas kernels, body(): pl.pallas_call(functools.partial(kernel, (n_e, n_c, n_r, n_q, rq, nz, ny)...  26 us
    unnamed x13, local copies, waits for them, and re-layouts  1.71 us
    convert_element_type x1, other arithmetic, body(): rounded = image.astype(BF16)  1 us
    sub x1, other arithmetic, body(): return image - total.reshape(shape) - penalty[:, :, :nz].reshape(shape)  0.84 us

profile of v2, /device:TPU:0, one launch (start us, length us, event | category | flops | bytes accessed | tf_op | source)
XLA Modules:
  0.0 30.9 jit_solution(551498469119820015)
XLA Ops:
  0.7 1.0 %convert_element_type.5 = bf16[48,1,2,2,192]{4,3,2,1,0:T(2,128)(2,1)S(1)} convert(f32[48,1,2,2,192]{4,3,2,1,0:T(2,128)} %param.14) | non-fusion elementwise | flops 36864 | bytes 221184 | tf_op jit(solution)/shard_map/convert_element_type | solution.py:362
  1.7 0.1 reshape.12.img_ref
  1.8 0.1 reshape.13
  2.0 0.0 copy-start
  2.0 0.0 copy-start.1
  2.0 0.0 copy-start.2
  2.1 0.8 %copy-done = bf16[4,96,54]{2,1,0:T(8,128)(2,1)S(1)} copy-done((bf16[4,96,54]{2,1,0:T(8,128)(2,1)S(1)}, bf16[4,96,54]{2,1,0:T(8,128)(2,1)}, u32[]{:S(2)}) %copy-start) | copy-done | bytes 41496
  2.9 0.0 copy-done.1
  2.9 0.0 copy-done.2
  2.9 26.0 %cascade.1 = (f32[48,768]{1,0:T(8,128)S(1)}, f32[48,4,256]{2,1,0:T(4,128)S(1)}) custom-call(f32[1]{0:T(128)S(6)} %copy.19.dc_ref, bf16[48,768]{1,0:T(8,128)(2,1)S(1)} %reshape.12.img_ref, bf16[6,16,4,256]{3,2,1,0:T(4,128)(2,1)S(1)} %fusion.11.xs_ref, bf16[2,2,192,384]{3,2,1,0:T(8,128)(2,1)} %bitcast.45, bf16[2,2,192,384]{3,2,1,0:T(8,128)(2,1)} %bitcast.46, ...), custom_call_target="tpu_custom_call" | custom-call | tf_op jit(solution)/shard_map/cascade/pallas_call | solution.py:392
  28.9 0.2 reshape.15
  29.1 0.0 copy-start.3
  29.1 0.2 reshape.14
  29.3 0.7 %copy-done.3 = f32[48,1,2,2,192]{4,3,2,1,0:T(2,128)S(1)} copy-done((f32[48,1,2,2,192]{4,3,2,1,0:T(2,128)S(1)}, f32[48,1,2,2,192]{4,3,2,1,0:T(2,128)}, u32[]{:S(2)}) %copy-start.3) | copy-done | bytes 147480
  30.0 0.8 %bitcast_subtract_fusion = f32[48,1,2,2,192]{4,3,2,1,0:T(2,128)} fusion(f32[48,1,2,2,192]{4,3,2,0,1:T(2,128)S(1)} %reshape.15, f32[48,1,2,2,192]{4,3,2,1,0:T(2,128)S(1)} %copy-done.3, f32[48,1,2,2,192]{4,3,2,0,1:T(2,128)S(1)} %reshape.14), kind=kLoop, calls=%fused_computation | loop fusion | flops 73728 | bytes 589824 | tf_op jit(solution)/shard_map/sub | solution.py:435
  (6 shorter events, 0.1 us)
Async XLA Ops:
  2.0 0.9 %copy-start = (bf16[4,96,54]{2,1,0:T(8,128)(2,1)S(1)}, bf16[4,96,54]{2,1,0:T(8,128)(2,1)}, u32[]{:S(2)}) copy-start(bf16[4,96,54]{2,1,0:T(8,128)(2,1)} %constant.14.clone.spread_ref) | copy-start | bytes 124420
  2.0 0.9 %copy-start.1 = (bf16[48,3,3,3,2]{0,4,3,2,1:T(2,128)(2,1)S(1)}, bf16[48,3,3,3,2]{0,4,3,2,1:T(2,128)(2,1)}, u32[]{:S(2)}) copy-start(bf16[48,3,3,3,2]{0,4,3,2,1:T(2,128)(2,1)} %param.15) | copy-start | bytes 15556
  2.0 0.9 %copy-start.2 = (f32[48]{0:T(128)S(1)}, f32[48]{0:T(128)}, u32[]{:S(2)}) copy-start(f32[48]{0:T(128)} %param.16) | copy-start | bytes 580
  29.1 0.9 %copy-start.3 = (f32[48,1,2,2,192]{4,3,2,1,0:T(2,128)S(1)}, f32[48,1,2,2,192]{4,3,2,1,0:T(2,128)}, u32[]{:S(2)}) copy-start(f32[48,1,2,2,192]{4,3,2,1,0:T(2,128)} %param.14) | copy-start | bytes 442372

commit v3 on v2

--- a/solution.py
+++ b/solution.py
@@ -36,10 +36,10 @@
 def kernel(
     cfg,
     dc_ref, img_ref, xs_ref, kspace_hbm, maps_hbm, samp_hbm, fz_hbm, az_hbm, ty_hbm,
-    filters_ref, spread_ref, thr_ref,
+    filters_ref, spread_hbm, thr_ref,
     adj_ref, pen_ref,
     gat, part, paired, rs_send, rs_recv, wide_ref, tall_ref, level, ext, edge, pen_send, pen_recv, pacc, slab,
-    kspace, maps, samp, fz, az, ty,
+    kspace, maps, samp, fz, az, ty, spread,
     local_sem, ag_send_sem, ag_recv_sem, x_send_sem, x_recv_sem, e_send_sem, e_recv_sem,
     p_send_sem, p_recv_sem, rs_send_sem, rs_recv_sem, f_send_sem, f_recv_sem, pair_send_sem, pair_recv_sem,
 ):
@@ -60,9 +60,12 @@
     loads = [
         pltpu.make_async_copy(src, dst, local_sem.at[i])
         for i, (src, dst) in enumerate(
-            [(kspace_hbm, kspace), (maps_hbm, maps), (samp_hbm, samp), (fz_hbm, fz), (az_hbm, az), (ty_hbm, ty)]
+            [(spread_hbm, spread), (kspace_hbm, kspace), (maps_hbm, maps), (samp_hbm, samp), (fz_hbm, fz), (az_hbm, az), (ty_hbm, ty)]
         )
     ]
+
+    for load in loads:
+        load.start()
 
     def remote(src, dst, send, recv, target):
         return pltpu.make_async_remote_copy(
@@ -128,14 +131,13 @@
 
     for d in range(chips):
         gather(d).start()
-    for load in loads:
-        load.start()
     gat[c] = img_ref[...]
 
     count = filters_ref.shape[-1]
     slices = s_local * n_r
     flat_filters = filters_ref[...].astype(F32).reshape(-1, count).astype(BF16)
-    pieces = [dot(spread_ref[at], flat_filters) for at in range(slices)]
+    loads[0].wait()
+    pieces = [dot(spread[at], flat_filters) for at in range(slices)]
     for at in range(slices):
         wide_ref[:, at * count : (at + 1) * count] = pieces[at].astype(BF16)
         tall_ref[at * count : (at + 1) * count, :] = pieces[at].T.astype(BF16)
@@ -247,7 +249,7 @@
     for d in range(1, chips):
         src = lax.rem(partner + n_c - 2 * d, n_c)
         remote(gat.at[src], gat.at[src], f_send_sem.at[d], f_recv_sem.at[d], (e, partner, r)).wait_recv()
-    for load in loads:
+    for load in loads[1:]:
         load.wait()
 
     def pair(s):
@@ -382,8 +384,8 @@
     m_view = jnp.transpose(coil_maps[:, 0], (1, 2, 3, 0))
     s_view = jnp.transpose(sampling[:, 0], (1, 0))
 
-    k_view, m_view, s_view, fz, az, ty = (
-        pltpu.with_memory_space_constraint(x, pltpu.HBM) for x in (k_view, m_view, s_view, fz, az, ty)
+    k_view, m_view, s_view, fz, az, ty, spread = (
+        pltpu.with_memory_space_constraint(x, pltpu.HBM) for x in (k_view, m_view, s_view, fz, az, ty, spread)
     )
     vmem = pl.BlockSpec(memory_space=pltpu.VMEM)
     hbm = pl.BlockSpec(memory_space=pltpu.HBM)
@@ -395,7 +397,7 @@
             jax.ShapeDtypeStruct((rb, s_local * width), F32),
             jax.ShapeDtypeStruct((rb, 2 * s_local, zp), F32),
         ),
-        in_specs=[smem, vmem, vmem, hbm, hbm, hbm, hbm, hbm, hbm, vmem, vmem, vmem],
+        in_specs=[smem, vmem, vmem, hbm, hbm, hbm, hbm, hbm, hbm, vmem, hbm, vmem],
         out_specs=(vmem, vmem),
         scratch_shapes=[
             pltpu.VMEM((n_c, rb, s_local * width), BF16),
@@ -418,7 +420,8 @@
             pltpu.VMEM(fz.shape, BF16),
             pltpu.VMEM(az.shape, BF16),
             pltpu.VMEM(ty.shape, BF16),
-            dma((6,)),
+            pltpu.VMEM(spread.shape, BF16),
+            dma((7,)),
             dma((n_c,)), dma((n_c,)),
             dma((peers,)), dma((peers,)),
             dma((2,)), dma((peers,)),

time: 31.1 us -> 30.9 us (level)
    unnamed x13 -> x11, local copies, waits for them, and re-layouts: 1.71 us -> 1.53 us
where the time goes in v3:
time: 30.9 us; the launch traced here: 30.7 us
  Pallas kernels  26 us (84%)
  local copies, waits for them, and re-layouts  2.1 us (7%)
  other arithmetic  1.84 us (6%)
  between operations  0.74 us (2%)
    pallas_call x1, Pallas kernels, body(): pl.pallas_call(functools.partial(kernel, (n_e, n_c, n_r, n_q, rq, nz, ny)...  26 us
    unnamed x11, local copies, waits for them, and re-layouts  1.53 us
    convert_element_type x1, other arithmetic, body(): rounded = image.astype(BF16)  1 us
    sub x1, other arithmetic, body(): return image - total.reshape(shape) - penalty[:, :, :nz].reshape(shape)  0.84 us

profile of v3, /device:TPU:0, one launch (start us, length us, event | category | flops | bytes accessed | tf_op | source)
XLA Modules:
  0.0 30.7 jit_solution(381423335028843065)
XLA Ops:
  0.7 1.0 %convert_element_type.5 = bf16[48,1,2,2,192]{4,3,2,1,0:T(2,128)(2,1)S(1)} convert(f32[48,1,2,2,192]{4,3,2,1,0:T(2,128)} %param.14) | non-fusion elementwise | flops 36864 | bytes 221184 | tf_op jit(solution)/shard_map/convert_element_type | solution.py:364
  1.7 0.1 reshape.12.img_ref
  1.8 0.1 reshape.13
  2.0 0.0 copy-start
  2.0 0.0 copy-start.1
  2.1 0.7 %copy-done = bf16[48,3,3,3,2]{0,4,3,2,1:T(2,128)(2,1)S(1)} copy-done((bf16[48,3,3,3,2]{0,4,3,2,1:T(2,128)(2,1)S(1)}, bf16[48,3,3,3,2]{0,4,3,2,1:T(2,128)(2,1)}, u32[]{:S(2)}) %copy-start) | copy-done | bytes 5208
  2.7 0.0 copy-done.1
  2.7 26.0 %cascade.1 = (f32[48,768]{1,0:T(8,128)S(1)}, f32[48,4,256]{2,1,0:T(4,128)S(1)}) custom-call(f32[1]{0:T(128)S(6)} %copy.19.dc_ref, bf16[48,768]{1,0:T(8,128)(2,1)S(1)} %reshape.12.img_ref, bf16[6,16,4,256]{3,2,1,0:T(4,128)(2,1)S(1)} %fusion.11.xs_ref, bf16[2,2,192,384]{3,2,1,0:T(8,128)(2,1)} %bitcast.45, bf16[2,2,192,384]{3,2,1,0:T(8,128)(2,1)} %bitcast.46, ...), custom_call_target="tpu_custom_call" | custom-call | tf_op jit(solution)/shard_map/cascade/pallas_call | solution.py:394
  28.8 0.2 reshape.15
  28.9 0.0 copy-start.2
  29.0 0.2 reshape.14
  29.1 0.7 %copy-done.2 = f32[48,1,2,2,192]{4,3,2,1,0:T(2,128)S(1)} copy-done((f32[48,1,2,2,192]{4,3,2,1,0:T(2,128)S(1)}, f32[48,1,2,2,192]{4,3,2,1,0:T(2,128)}, u32[]{:S(2)}) %copy-start.2) | copy-done | bytes 147480
  29.9 0.8 %bitcast_subtract_fusion = f32[48,1,2,2,192]{4,3,2,1,0:T(2,128)} fusion(f32[48,1,2,2,192]{4,3,2,0,1:T(2,128)S(1)} %reshape.15, f32[48,1,2,2,192]{4,3,2,1,0:T(2,128)S(1)} %copy-done.2, f32[48,1,2,2,192]{4,3,2,0,1:T(2,128)S(1)} %reshape.14), kind=kLoop, calls=%fused_computation | loop fusion | flops 73728 | bytes 589824 | tf_op jit(solution)/shard_map/sub | solution.py:438
  (6 shorter events, 0.1 us)
Async XLA Ops:
  2.0 0.7 %copy-start = (bf16[48,3,3,3,2]{0,4,3,2,1:T(2,128)(2,1)S(1)}, bf16[48,3,3,3,2]{0,4,3,2,1:T(2,128)(2,1)}, u32[]{:S(2)}) copy-start(bf16[48,3,3,3,2]{0,4,3,2,1:T(2,128)(2,1)} %param.15) | copy-start | bytes 15556
  2.0 0.7 %copy-start.1 = (f32[48]{0:T(128)S(1)}, f32[48]{0:T(128)}, u32[]{:S(2)}) copy-start(f32[48]{0:T(128)} %param.16) | copy-start | bytes 580
  28.9 0.9 %copy-start.2 = (f32[48,1,2,2,192]{4,3,2,1,0:T(2,128)S(1)}, f32[48,1,2,2,192]{4,3,2,1,0:T(2,128)}, u32[]{:S(2)}) copy-start(f32[48,1,2,2,192]{4,3,2,1,0:T(2,128)} %param.14) | copy-start | bytes 442372
